TPU v7x, 32 devices: a whole 2x2x4 slice. The times are simulated.
32 devices in a mesh: wide: 2 (over x), grow: 4 (over y, core), gcol: 4 (over z).
Axes of the slice: x: 2, y: 2, z: 4, core: 2. Of those that a mesh axis runs over, the one named last changes fastest.
Arguments:
- diag_block: float32 [2, 1024, 1024], P('wide', ('grow', 'gcol')), as said below
- lower_block: float32 [2, 3072, 1024], P('wide', ('grow', 'gcol')), may hold values from -0.1875 to 0.1875
- trailing_block: float32 [2, 3072, 3072], P('wide', 'grow', 'gcol'), as said below
- parent_front: float32 [4, 2048, 8192], P('grow', 'wide', 'gcol'), may hold values from -3 to 3
- row_map: int32 [2, 24], replicated, may hold values from 0 to 63, as said below
Outputs:
- factor: float32 [2, 1024, 1024], P('wide', ('grow', 'gcol'))
- panel: float32 [2, 3072, 1024], P('wide', ('grow', 'gcol'))
- parent: float32 [4, 2048, 8192], P('grow', 'wide', 'gcol')
Inputs may be any that keep to these rules, and one draw needn't show every extreme that they name: Each diag_block[g] is symmetric and positive definite. Each trailing_block[g] is symmetric. `row_map`: the blocks of one child are distinct, and child block b goes to a grandparent block p with p // 16 equal to b // 6.
All inputs are finite; a program needn't handle non-finite values.
Results may differ from a plain program's by a relative error of at most 0.0003.
Values sent between devices are 32-bit elements; how exact they have to be, the bound alone decides.
A program may use at most 128 MiB of HBM per device.

v0:
```python
import functools
import math

import jax
import jax.numpy as jnp
from jax import lax
from jax.experimental import pallas as pl
from jax.experimental.pallas import tpu as pltpu
from jax.sharding import PartitionSpec as P

BLOCK = 128
HALF = 64
F32 = jnp.float32
BF16 = jnp.bfloat16
NT = (((1,), (1,)), ((), ()))
NN = (((1,), (0,)), ((), ()))
VMEM = pl.BlockSpec(memory_space=pltpu.VMEM)
SMEM = pl.BlockSpec(memory_space=pltpu.SMEM)


def full_dot(a, b, dims):
    return lax.dot_general(
        a, b, dims, precision=lax.Precision.HIGHEST, preferred_element_type=F32
    )


def parts(x):
    high = x.astype(BF16)
    return high, (x - high.astype(F32)).astype(BF16)


def split_dot(a, b, dims):
    one = functools.partial(lax.dot_general, dimension_numbers=dims, preferred_element_type=F32)
    return one(a[0], b[0]) + (one(a[0], b[1]) + one(a[1], b[0]))


def factor_half(block):
    half = block.shape[0]
    rows = lax.broadcasted_iota(jnp.int32, (half, half), 0)
    cols = lax.broadcasted_iota(jnp.int32, (half, half), 1)
    eye = jnp.where(rows == cols, 1.0, 0.0).astype(F32)
    full = jnp.concatenate([block, eye], axis=1)
    count = half // 8
    wide = (8, 2 * half)
    groups = [full[8 * s : 8 * s + 8] for s in range(count)]
    sub = lax.broadcasted_iota(jnp.int32, wide, 0)
    at_row = [jnp.full(wide, i, jnp.int32) for i in range(8)]
    spread = lambda x: jnp.broadcast_to(x, wide)
    take = lambda x, i: jnp.take_along_axis(x, at_row[i], axis=0, mode="promise_in_bounds")
    done = []
    for s in range(count):
        c = 8 * s
        column = {
            t: [spread(groups[t][:, c + j : c + j + 1]) for j in range(8)] for t in range(s, count)
        }
        lead = [spread(groups[s][i : i + 1, :]) for i in range(8)]
        pivot = {(i, j): take(column[s][j], i) for i in range(8) for j in range(i, 8)}
        below = range(s + 1, count)
        keep = jnp.zeros(wide, F32)
        for j in range(8):
            r = lax.rsqrt(pivot[j, j])
            unit = lead[j] * r
            mult = {i: pivot[j, i] * r for i in range(j + 1, 8)}
            for i in range(j + 1, 8):
                for q in range(i, 8):
                    pivot[i, q] = pivot[i, q] - mult[i] * mult[q]
                lead[i] = lead[i] - mult[i] * unit
            for t in below:
                m = column[t][j] * r
                for i in range(j + 1, 8):
                    column[t][i] = column[t][i] - m * mult[i]
                groups[t] = groups[t] - m * unit
            keep = jnp.where(sub == j, unit, keep)
        done.append(keep)
    both = jnp.concatenate(done, axis=0)
    upper = jnp.where(rows <= cols, both[:, :half], 0.0)
    inverse = jnp.where(rows >= cols, both[:, half:], 0.0)
    return upper.T, inverse


def square(a, b, c):
    return jnp.concatenate(
        [
            jnp.concatenate([a, jnp.zeros_like(a)], axis=1),
            jnp.concatenate([b, c], axis=1),
        ],
        axis=0,
    )


def factor_in_place(a, w, lh, ll, between):
    n = a.shape[0]
    count = n // BLOCK

    def step(k, carry):
        o = pl.multiple_of(k * BLOCK, BLOCK)
        d = a[pl.ds(o, BLOCK), pl.ds(o, BLOCK)]
        l1, w1 = factor_half(d[:HALF, :HALF])
        l21 = full_dot(d[HALF:, :HALF], w1, NT)
        l2, w2 = factor_half(d[HALF:, HALF:] - full_dot(l21, l21, NT))
        w21 = -full_dot(w2, full_dot(l21, w1, NN), NN)
        a[pl.ds(o, BLOCK), pl.ds(o, BLOCK)] = square(l1, l21, l2)
        w[k] = square(w1, w21, w2)
        for at in range(count - 1):

            @pl.when(k == at)
            def _(at=at):
                low, high = at * BLOCK, at * BLOCK + BLOCK
                a[low:high, high:] = jnp.zeros((BLOCK, n - high), F32)
                p = split_dot(parts(a[high:, low:high]), parts(w[at]), NT)
                a[high:, low:high] = p
                lh[high:, low:high], ll[high:, low:high] = parts(p)
                end = min(high + (1 + at % 2) * BLOCK, n)
                start = 0 if at % 2 else low
                left, right = slice(high, n), slice(high, end)
                a[high:, high:end] = a[high:, high:end] - split_dot(
                    (lh[left, start:high], ll[left, start:high]),
                    (lh[right, start:high], ll[right, start:high]),
                    NT,
                )
                for act in between.get(at, ()):
                    act()

        return carry

    lax.fori_loop(0, count, step, 0)


def most_slots(blocks, per_owner):
    return min(blocks, per_owner)


def invert_diagonal(l_ref, w_ref, wh, wl):
    group = wh.shape[1]

    def inverse(at, size):
        if size == BLOCK:
            return w_ref[at // BLOCK]
        cut = size // 2
        first, second = inverse(at, cut), inverse(at + cut, cut)
        across = l_ref[at + cut : at + size, at : at + cut]
        product = parts(split_dot(parts(across), parts(first), NN))
        return square(first, -split_dot(parts(second), product, NN), second)

    for k in range(wh.shape[0]):
        wh[k], wl[k] = parts(inverse(k * group, group))


def front_kernel(
    rows, columns, owners, sure, quarter, map_ref, d_ref, x_ref, t_ref,
    factor_ref, panel_ref, piece_ref, need_ref,
    a, w, br, bc, xh, xl, yh, yl, lh, ll, wh, wl, t, stage, x_send, x_recv,
    local, line_send, line_recv, far_send, far_recv, near_send, near_recv,
    b_send, b_recv, c_send, c_recv,
):
    child = lax.axis_index("wide")
    row, column = lax.axis_index("grow"), lax.axis_index("gcol")
    n = a.shape[1]
    grain = br.shape[1]
    q = br.shape[0] * grain
    blocks = q // BLOCK
    per_owner = quarter // owners
    far_row = lax.rem(row + rows // 2, rows)
    near_row = row + 1 - 2 * lax.rem(row, 2)
    near_far_row = lax.rem(near_row + rows // 2, rows)
    right, left = {"gcol": column + 1}, {"gcol": column - 1}
    far, near = {"grow": far_row}, {"grow": near_row}
    share = d_ref.shape[0]
    grains = x_ref.shape[0]
    part = grains * grain
    has_left, has_right = column > 0, column < columns - 1

    def band(r, c):
        return pl.ds(pl.multiple_of((r * columns + c) * share, share), share)

    def cells(r, c, act):
        outer = (r == 0) | (r == rows - 1)
        start = jnp.where(outer, n // 2, jnp.where(r < rows // 2, 0, n // 4))
        act(0, a.at[band(r, c), pl.ds(pl.multiple_of(start, n // 4), n // 2)])
        extra = jnp.where(r == 0, 0, n // 4)
        slim = a.at[band(r, c), pl.ds(pl.multiple_of(extra, n // 4), n // 4)]
        pl.when(outer)(functools.partial(act, 1, slim))

    def remote(ref, send, recv, to):
        return pltpu.make_async_remote_copy(
            src_ref=ref, dst_ref=ref, send_sem=send, recv_sem=recv,
            device_id=to, device_id_type=pl.DeviceIdType.MESH,
        )

    own_d = pltpu.make_async_copy(d_ref, a.at[band(row, column)], local.at[0])
    own_x = pltpu.make_async_copy(x_ref, br.at[pl.ds(column * grains, grains)], local.at[1])
    own_t = pltpu.make_async_copy(t_ref, t, local.at[2])
    own_d.start()
    own_x.start()
    own_t.start()
    barrier = pltpu.get_barrier_semaphore()
    next_column = {"gcol": lax.rem(column + 1, columns)}
    last_column = {"gcol": lax.rem(column + columns - 1, columns)}
    others = [{"wide": lax.rem(child + d, owners)} for d in range(1, owners)]
    for to in [far, near, next_column, last_column] + others:
        pl.semaphore_signal(barrier, inc=1, device_id=to, device_id_type=pl.DeviceIdType.MESH)
    pl.semaphore_wait(barrier, 3 + owners)
    own_d.wait()
    own_x.wait()

    def pass_on(ref, send, recv, c):
        @pl.when((c <= column) & has_right)
        def _():
            remote(ref, send.at[0, c], recv.at[c], right).start()

        @pl.when((c >= column) & has_left)
        def _():
            remote(ref, send.at[1, c], recv.at[c], left).start()

    def passed(ref, send, recv, c):
        @pl.when((c <= column) & has_right)
        def _():
            remote(ref, send.at[0, c], recv.at[c], right).wait_send()

        @pl.when((c >= column) & has_left)
        def _():
            remote(ref, send.at[1, c], recv.at[c], left).wait_send()

    def at_distance(d, act):
        for c, there in ((column - d, column - d >= 0), (column + d, column + d < columns)):
            pl.when(there)(functools.partial(act, c))

    def spread(c):
        def act(i, ref):
            pass_on(ref, line_send.at[i], line_recv.at[i], c)
            remote(ref, far_send.at[i, c], far_recv.at[i, c], far).start()
            remote(ref, near_send.at[i, 0, c], near_recv.at[i, 0, c], near).start()

        cells(row, c, act)

    def arrived(c):
        def act(i, ref):
            remote(ref, line_send.at[i, 0, c], line_recv.at[i, c], right).wait_recv()

        cells(row, c, act)
        spread(c)

    def crossed(c):
        def act(i, ref):
            remote(ref, far_send.at[i, c], far_recv.at[i, c], far).wait_recv()
            remote(ref, near_send.at[i, 1, c], near_recv.at[i, 1, c], near).start()

        cells(far_row, c, act)

    def shared(c):
        def direct(i, ref):
            remote(ref, near_send.at[i, 0, c], near_recv.at[i, 0, c], near).wait_recv()

        def passed_on(i, ref):
            remote(ref, near_send.at[i, 1, c], near_recv.at[i, 1, c], near).wait_recv()

        cells(near_row, c, direct)
        cells(near_far_row, c, passed_on)

    def sent(c):
        def mine(i, ref):
            remote(ref, far_send.at[i, c], far_recv.at[i, c], far).wait_send()
            remote(ref, near_send.at[i, 0, c], near_recv.at[i, 0, c], near).wait_send()
            passed(ref, line_send.at[i], line_recv.at[i], c)

        def relayed(i, ref):
            remote(ref, near_send.at[i, 1, c], near_recv.at[i, 1, c], near).wait_send()

        cells(row, c, mine)
        cells(far_row, c, relayed)

    root = row == column
    relay = far_row == column
    from_near = jnp.logical_not(root | relay)

    def piece(ref, c, h):
        return ref.at[pl.ds(c * grains + h, 1)]

    def give(c, h):
        @pl.when(root)
        def _():
            for slot, to in ((0, far), (1, near)):
                pltpu.make_async_remote_copy(
                    src_ref=piece(br, c, h), dst_ref=piece(bc, c, h),
                    send_sem=c_send.at[h, slot, c], recv_sem=c_recv.at[h, c],
                    device_id=to, device_id_type=pl.DeviceIdType.MESH,
                ).start()

    def start_line():
        for h in range(grains):
            pass_on(piece(br, column, h), b_send.at[h], b_recv.at[h], column)

    def take(c, start=0, stop=3):
        for h in range(grains * start // 3, grains * stop // 3):
            remote(piece(br, c, h), b_send.at[h, 0, c], b_recv.at[h, c], right).wait_recv()
            pass_on(piece(br, c, h), b_send.at[h], b_recv.at[h], c)
            give(c, h)

    def forward(c, start=0, stop=3):
        @pl.when(relay)
        def _():
            for h in range(grains * start // 3, grains * stop // 3):
                remote(piece(bc, c, h), c_send.at[h, 0, c], c_recv.at[h, c], far).wait_recv()
                remote(piece(bc, c, h), c_send.at[h, 1, c], c_recv.at[h, c], near).start()

    spread(column)
    inside = has_left & has_right
    at_distance(1, arrived)
    crossed(column)
    for d in range(2, columns):
        at_distance(d, arrived)
        if d == max(columns - 2, 2):
            start_line()
        at_distance(d - 1, crossed)
    at_distance(columns - 1, crossed)
    for c in range(columns):
        shared(c)
    for c in range(columns):
        sent(c)
    for h in range(grains):
        give(column, h)
    for i in range(n // 2, n, BLOCK):
        for j in range(0, n // 4, BLOCK):
            a[i : i + BLOCK, j : j + BLOCK] = a[j : j + BLOCK, i : i + BLOCK].T

    between = {}
    some = lambda start, stop: functools.partial(take, start=start, stop=stop)
    between[1] = [functools.partial(at_distance, 1, take)]
    between[2] = [functools.partial(forward, column)]
    between[4] = [functools.partial(at_distance, 2, some(0, 2)), functools.partial(at_distance, 1, forward)]
    between[5] = [functools.partial(at_distance, 2, some(2, 3))]
    factor_in_place(a, w, lh, ll, between)
    factor_ref[...] = a[band(row, column), :]
    invert_diagonal(a, w, wh, wl)
    for d in range(3, columns - 1):
        at_distance(d, take)
        at_distance(d, forward)
    group = wh.shape[1]
    cut = group // 2

    def solve(i, carry):
        step = (i + 1) // 2
        inner = jnp.where(i % 2 == 1, column - step, column + step)
        outer = jnp.where(2 * column < columns, i, columns - 1 - i)
        c = jnp.where(i <= 2 * jnp.minimum(column, columns - 1 - column), inner, outer)
        at = pl.ds(c * grains, grains)
        def events(*acts):
            for d, act in acts:
                if d == 2 or d > 2 and d == columns - 1:
                    at_distance(d, act)

        some_on = lambda start, stop: functools.partial(forward, start=start, stop=stop)
        last = max(columns - 1, 3)
        pl.when(i == 0)(lambda: events((last, some(0, 1))))
        pl.when(i == 1)(lambda: events((2, forward), (last, some(1, 2))))
        pl.when(i == 2)(lambda: events((last, some(2, 3)), (last, some_on(0, 1))))
        pl.when(i == 3)(lambda: events((last, some_on(1, 3))))

        @pl.when(from_near)
        def _():
            for h in range(grains):
                remote(piece(bc, c, h), c_send.at[h, 0, c], c_recv.at[h, c], near).wait_recv()

        @pl.when(root)
        def _():
            bc[at] = br[at]

        for k in range(n // group):
            low, high = k * group, (k + 1) * group
            both = lambda y, x, cut: jnp.concatenate(
                [ref[at, :, cut].reshape(part, cut.stop - cut.start) for ref in (y, x)], axis=0
            )
            rest = both(br, bc, slice(low, high))
            if low:
                done = slice(0, low)
                rest = rest - split_dot(
                    (both(yh, xh, done), both(yl, xl, done)),
                    (lh[low:high, :low], ll[low:high, :low]),
                    NT,
                )
            rest = parts(rest)
            early = split_dot(
                tuple(z[:, :cut] for z in rest), (wh[k, :cut, :cut], wl[k, :cut, :cut]), NT
            )
            late = split_dot(rest, (wh[k, cut:, :], wl[k, cut:, :]), NT)
            for x, start in ((early, low), (late, low + cut)):
                stop = start + cut
                for (y_to, x_to), value in zip(((yh, xh), (yl, xl)), parts(x)):
                    y_to[at, :, start:stop] = value[:part].reshape(grains, grain, cut)
                    x_to[at, :, start:stop] = value[part:].reshape(grains, grain, cut)

                @pl.when(i == 0)
                def _(x=x, start=start, stop=stop):
                    panel_ref[:, start:stop] = x[:part]

        return carry

    lax.fori_loop(0, columns, solve, 0)
    own_t.wait()

    def owner(g, r, b):
        return (map_ref[g, r * blocks + b] % quarter) // per_owner

    mine = [owner(child, row, b) for b in range(blocks)]

    def pick(to, slot):
        block, rank = jnp.int32(0), jnp.int32(0)
        for b in range(blocks):
            here = mine[b] == to
            block = jnp.where(here & (rank == slot), b, block)
            rank += here.astype(jnp.int32)
        return block

    def give_away(s, d):
        return pltpu.make_async_remote_copy(
            src_ref=stage.at[s], dst_ref=piece_ref.at[blocks + s],
            send_sem=x_send.at[s], recv_sem=x_recv.at[s],
            device_id={"wide": lax.rem(child + d, owners)}, device_id_type=pl.DeviceIdType.MESH,
        )

    slots = [(d, i) for d in range(1, owners) for i in range(sure)]
    picked = [pick(lax.rem(child + d, owners), i) for d, i in slots]
    each = BLOCK // grain
    columns_side = tuple(x[...].reshape(q, n) for x in (xh, xl))
    for first in range(0, len(slots), 2):
        group = picked[first : first + 2]
        sides = tuple(
            jnp.concatenate([y[block * each + h] for block in group for h in range(each)], axis=0)
            for y in (yh, yl)
        )
        product = split_dot(sides, columns_side, NT)
        for e, block in enumerate(group):
            stage[first + e] = t[block] - product[e * BLOCK : e * BLOCK + BLOCK, :]
            give_away(first + e, slots[first + e][0]).start()
    step = 3 if blocks % 3 == 0 else 1
    for first in range(0, blocks, step):
        rows_side = tuple(
            y[first * each : (first + step) * each].reshape(step * BLOCK, n) for y in (yh, yl)
        )
        product = split_dot(rows_side, columns_side, NT)
        for e in range(step):
            piece_ref[first + e] = t[first + e] - product[e * BLOCK : e * BLOCK + BLOCK, :]
    for c in range(columns):
        for h in range(grains):

            @pl.when(relay)
            def _(c=c, h=h):
                remote(piece(bc, c, h), c_send.at[h, 1, c], c_recv.at[h, c], near).wait_send()

            @pl.when(root)
            def _(c=c, h=h):
                remote(piece(br, c, h), c_send.at[h, 0, c], c_recv.at[h, c], far).wait_send()
                remote(piece(br, c, h), c_send.at[h, 1, c], c_recv.at[h, c], near).wait_send()

            passed(piece(br, c, h), b_send.at[h], b_recv.at[h], c)
    need = jnp.int32(0)
    if sure < most_slots(blocks, per_owner):
        for g in range(owners):
            for r in range(rows):
                there = [owner(g, r, b) for b in range(blocks)]
                for e in range(owners):
                    if e != g:
                        need = jnp.maximum(need, sum((x == e).astype(jnp.int32) for x in there))
    need_ref[0] = need
    for s, (d, _) in enumerate(slots):
        give_away(s, d).wait()


def front_call(row_map, diag, lower, trailing, rows, columns, owners, sure, quarter):
    n = diag.shape[1]
    share, part = diag.shape[0], lower.shape[0]
    q = part * columns
    blocks = q // BLOCK
    dma = pltpu.SemaphoreType.DMA
    away = (owners - 1) * sure
    grain = math.gcd(part, BLOCK)
    grains = part // grain
    group = math.gcd(n, 4 * BLOCK)
    return pl.pallas_call(
        functools.partial(front_kernel, rows, columns, owners, sure, quarter),
        name="front",
        out_shape=(
            jax.ShapeDtypeStruct((share, n), F32),
            jax.ShapeDtypeStruct((part, n), F32),
            jax.ShapeDtypeStruct((blocks + away, BLOCK, q), F32),
            jax.ShapeDtypeStruct((1,), jnp.int32),
        ),
        in_specs=[SMEM] + [pl.BlockSpec(memory_space=pl.ANY)] * 3,
        out_specs=(VMEM,) * 3 + (SMEM,),
        scratch_shapes=[
            pltpu.VMEM((n, n), F32),
            pltpu.VMEM((n // BLOCK, BLOCK, BLOCK), F32),
            pltpu.VMEM((q // grain, grain, n), F32),
            pltpu.VMEM((q // grain, grain, n), F32),
            pltpu.VMEM((q // grain, grain, n), BF16),
            pltpu.VMEM((q // grain, grain, n), BF16),
            pltpu.VMEM((q // grain, grain, n), BF16),
            pltpu.VMEM((q // grain, grain, n), BF16),
            pltpu.VMEM((n, n), BF16),
            pltpu.VMEM((n, n), BF16),
            pltpu.VMEM((n // group, group, group), BF16),
            pltpu.VMEM((n // group, group, group), BF16),
            pltpu.VMEM((blocks, BLOCK, q), F32),
            pltpu.VMEM((away, BLOCK, q), F32),
            dma((away,)), dma((away,)),
            dma((3,)), dma((2, 2, columns)), dma((2, columns)), dma((2, columns)), dma((2, columns)),
            dma((2, 2, columns)), dma((2, 2, columns)),
            dma((grains, 2, columns)), dma((grains, columns)),
            dma((grains, 2, columns)), dma((grains, columns)),
        ],
        compiler_params=pltpu.CompilerParams(
            vmem_limit_bytes=56 << 20, collective_id=0, has_side_effects=True
        ),
    )(
        row_map, diag, lower.reshape(part // grain, grain, n), trailing.reshape(blocks, BLOCK, q)
    )


def rest_kernel(owners, sure, more, quarter, map_ref, piece_ref, out_ref, stage, send, recv):
    child, row = lax.axis_index("wide"), lax.axis_index("grow")
    blocks = out_ref.shape[2] // BLOCK
    per_owner = quarter // owners
    barrier = pltpu.get_barrier_semaphore()
    for d in range(1, owners):
        pl.semaphore_signal(
            barrier, inc=1, device_id={"wide": lax.rem(child + d, owners)},
            device_id_type=pl.DeviceIdType.MESH,
        )
    mine = [(map_ref[child, row * blocks + b] % quarter) // per_owner for b in range(blocks)]

    def give_away(s, d):
        return pltpu.make_async_remote_copy(
            src_ref=stage.at[s], dst_ref=out_ref.at[s], send_sem=send.at[s], recv_sem=recv.at[s],
            device_id={"wide": lax.rem(child + d, owners)}, device_id_type=pl.DeviceIdType.MESH,
        )

    slots = [(d, sure + i) for d in range(1, owners) for i in range(more)]
    for s, (d, slot) in enumerate(slots):
        block, rank = jnp.int32(0), jnp.int32(0)
        for b in range(blocks):
            here = mine[b] == lax.rem(child + d, owners)
            block = jnp.where(here & (rank == slot), b, block)
            rank += here.astype(jnp.int32)
        stage[s] = piece_ref[block]
    pl.semaphore_wait(barrier, owners - 1)
    for s, (d, _) in enumerate(slots):
        give_away(s, d).start()
    for s, (d, _) in enumerate(slots):
        give_away(s, d).wait()


def rest_call(row_map, pieces, owners, sure, more, quarter):
    away = (owners - 1) * more
    shape = (away,) + pieces.shape[1:]
    dma = pltpu.SemaphoreType.DMA
    return pl.pallas_call(
        functools.partial(rest_kernel, owners, sure, more, quarter),
        name="rest",
        out_shape=jax.ShapeDtypeStruct(shape, F32),
        in_specs=[SMEM, VMEM],
        out_specs=VMEM,
        scratch_shapes=[pltpu.VMEM(shape, F32), dma((away,)), dma((away,))],
        compiler_params=pltpu.CompilerParams(
            vmem_limit_bytes=12 << 20, collective_id=more, has_side_effects=True
        ),
    )(row_map, pieces)


def add_kernel(owners, sure, more, map_ref, parent_ref, factor_ref, panel_ref, *refs):
    pieces = refs[:-6]
    out_ref, factor_out, panel_out, total, read, write = refs[-6:]
    per_owner = total.shape[0] // BLOCK
    quarter = owners * per_owner
    q = pieces[0].shape[2]
    blocks = q // BLOCK
    column_blocks = total.shape[1] // BLOCK
    child, row = lax.axis_index("wide"), lax.axis_index("grow")
    column = lax.axis_index("gcol")

    def rows_of(p):
        return pl.ds(pl.multiple_of(p * BLOCK, BLOCK), BLOCK)

    def fetch(p):
        return pltpu.make_async_copy(parent_ref.at[rows_of(p)], total.at[rows_of(p)], read.at[p])

    def store(p):
        return pltpu.make_async_copy(total.at[rows_of(p)], out_ref.at[rows_of(p)], write.at[p])

    for p in range(per_owner):
        fetch(p).start()
    others = (
        pltpu.make_async_copy(factor_ref, factor_out, write.at[per_owner]),
        pltpu.make_async_copy(panel_ref, panel_out, write.at[per_owner + 1]),
    )

    def add_rows(p, carry):
        fetch(p).wait()

        def add(g, carry):
            block, slot, rank = jnp.int32(-1), jnp.int32(-1), jnp.int32(0)
            for b in range(blocks):
                to = map_ref[g, row * blocks + b] % quarter
                hit = to == child * per_owner + p
                block = jnp.where(hit, b, block)
                slot = jnp.where(hit, rank, slot)
                rank += (to // per_owner == child).astype(jnp.int32)
            away = lax.rem(child - g + owners, owners) - 1

            def put(ref, index):
                for b in range(blocks):
                    to = map_ref[g, column * blocks + b] % column_blocks
                    at = pl.ds(pl.multiple_of(to * BLOCK, BLOCK), BLOCK)
                    total[rows_of(p), at] += ref[index, :, b * BLOCK : b * BLOCK + BLOCK]

            @pl.when((block >= 0) & ((g == child) | (slot < sure)))
            def _():
                put(pieces[0], jnp.where(g == child, block, blocks + away * sure + slot))

            if len(pieces) > 1:

                @pl.when((block >= 0) & (g != child) & (slot >= sure))
                def _():
                    put(pieces[1], away * more + slot - sure)

            return carry

        lax.fori_loop(0, owners, add, 0)
        store(p).start()
        return carry

    lax.fori_loop(0, per_owner, add_rows, 0)
    for copy in others:
        copy.start()
    for p in range(per_owner):
        store(p).wait()
    for copy in others:
        copy.wait()


def add_call(row_map, parent, factor, panel, pieces, owners, sure, more):
    dma = pltpu.SemaphoreType.DMA
    per_owner = parent.shape[0] // BLOCK
    anywhere = pl.BlockSpec(memory_space=pl.ANY)
    return pl.pallas_call(
        functools.partial(add_kernel, owners, sure, more),
        name="extend_add",
        out_shape=tuple(jax.ShapeDtypeStruct(x.shape, F32) for x in (parent, factor, panel)),
        in_specs=[SMEM, anywhere] + [VMEM] * (2 + len(pieces)),
        out_specs=(anywhere,) * 3,
        scratch_shapes=[pltpu.VMEM(parent.shape, F32), dma((per_owner,)), dma((per_owner + 2,))],
        compiler_params=pltpu.CompilerParams(vmem_limit_bytes=24 << 20),
    )(row_map, parent, factor, panel, *pieces)


def body(diag_block, lower_block, trailing_block, parent_front, row_map):
    owners = lax.axis_size("wide")
    rows, columns = lax.axis_size("grow"), lax.axis_size("gcol")
    quarter = parent_front.shape[1] * owners // BLOCK
    blocks = trailing_block.shape[1] // BLOCK
    most = most_slots(blocks, quarter // owners)
    sure = max(1, 2 * most // 3)
    factor, panel, pieces, need = front_call(
        row_map, diag_block[0], lower_block[0], trailing_block[0], rows, columns, owners, sure, quarter,
    )

    def finish(more):
        def run():
            extra = (rest_call(row_map, pieces, owners, sure, more, quarter),) if more else ()
            return add_call(
                row_map, parent_front[0], factor, panel, (pieces,) + extra, owners, sure, more
            )

        return run

    branches = [finish(more) for more in range(most - sure + 1)]
    parent, factor, panel = lax.switch(jnp.clip(need[0] - sure, 0, most - sure), branches)
    return (factor[None], panel[None], parent[None])


def solution(mesh):
    placed = (
        P("wide", ("grow", "gcol"), None),
        P("wide", ("grow", "gcol"), None),
        P("wide", "grow", "gcol"),
        P("grow", "wide", "gcol"),
        P(),
    )
    return jax.shard_map(
        body,
        mesh=mesh,
        in_specs=placed,
        out_specs=(
            P("wide", ("grow", "gcol"), None),
            P("wide", ("grow", "gcol"), None),
            P("grow", "wide", "gcol"),
        ),
        check_vma=False,
    )
```

profile of v0, /device:TPU:4, one launch (start us, length us, event | category | flops | bytes accessed | tf_op | source)
XLA Modules:
  0.0 140.6 jit_solution(8218028388825469061)
XLA Ops:
  0.6 119.1 %front.1 = (f32[64,1024]{1,0:T(8,128)S(1)}, f32[192,1024]{1,0:T(8,128)S(1)}, f32[10,128,768]{2,1,0:T(8,128)S(1)}, s32[1]{0:T(128)}) custom-call(s32[2,24]{1,0:T(2,128)} %map_ref.1, f32[64,1024]{1,0:T(8,128)} %bitcast.21, f32[3,64,1024]{2,1,0:T(8,128)} %bitcast.20, f32[6,128,768]{2,1,0:T(8,128)} %bitcast.19), custom_call_target="tpu_custom_call" | custom-call | tf_op jit(solution)/shard_map/front/pallas_call | solution.py:479
  120.3 20.2 %conditional.1 = (f32[1,64,1024]{2,1,0:T(8,128)}, f32[1,192,1024]{2,1,0:T(8,128)}, f32[1,1024,2048]{2,1,0:T(8,128)}) conditional(s32[]{:T(128)} %bitcast.15, (f32[1,1024,2048]{2,1,0:T(8,128)}, s32[2,24]{1,0:T(2,128)}, f32[64,1024]{1,0:T(8,128)S(1)}, f32[192,1024]{1,0:T(8,128)S(1)}, f32[10,128,768]{2,1,0:T(8,128)S(1)}) %tuple.30, ...), branch_computations={%region_0.1_spmd, %region_1.2_spmd, %region_2.3_spmd} | conditional | bytes 24 | solution.py:676
  120.3 12.4 %rest.2.refs_1_ = f32[1,128,768]{2,1,0:T(8,128)S(1)} custom-call(s32[2,24]{1,0:T(2,128)} %get-tuple-element.51.map_ref, f32[10,128,768]{2,1,0:T(8,128)S(1)} %get-tuple-element.55.piece_ref.refs_0_), custom_call_target="tpu_custom_call" | custom-call | tf_op jit(solution)/shard_map/cond/branch_1_fun/rest/pallas_call | solution.py:556
  132.7 7.7 %extend_add.4 = (f32[1024,2048]{1,0:T(8,128)}, f32[64,1024]{1,0:T(8,128)}, f32[192,1024]{1,0:T(8,128)}) custom-call(s32[2,24]{1,0:T(2,128)} %get-tuple-element.51.map_ref, f32[1024,2048]{1,0:T(8,128)} %bitcast.17, f32[64,1024]{1,0:T(8,128)S(1)} %get-tuple-element.53.factor_ref, f32[192,1024]{1,0:T(8,128)S(1)} %get-tuple-element.54.panel_ref, ...), custom_call_target="tpu_custom_call" | custom-call | tf_op jit(solution)/shard_map/cond/branch_1_fun/extend_add/pallas_call | solution.py:644
where the time goes:
time: 141 us
  Pallas kernels  139 us (99%)
    pallas_call x1, Pallas kernels, front_call(): pl.pallas_call(functools.partial(front_kernel, rows, columns, owners, sur...  119 us
    pallas_call x1, Pallas kernels, rest_call(): pl.pallas_call(functools.partial(rest_kernel, owners, sure, more, quarter...  12.4 us
    pallas_call x1, Pallas kernels, add_call(): pl.pallas_call(functools.partial(add_kernel, owners, sure, more), name='e...  7.73 us

commit v1 on v0

--- a/solution.py
+++ b/solution.py
@@ -147,8 +147,8 @@
 
 
 def front_kernel(
-    rows, columns, owners, sure, quarter, map_ref, d_ref, x_ref, t_ref,
-    factor_ref, panel_ref, piece_ref, need_ref,
+    rows, columns, owners, sure, quarter, map_ref, d_ref, x_ref, t_ref, parent_ref,
+    factor_ref, panel_ref, piece_ref, held_ref, need_ref,
     a, w, br, bc, xh, xl, yh, yl, lh, ll, wh, wl, t, stage, x_send, x_recv,
     local, line_send, line_recv, far_send, far_recv, near_send, near_recv,
     b_send, b_recv, c_send, c_recv,
@@ -193,6 +193,7 @@
     own_d.start()
     own_x.start()
     own_t.start()
+    own_p = pltpu.make_async_copy(parent_ref, held_ref, local.at[3])
     barrier = pltpu.get_barrier_semaphore()
     next_column = {"gcol": lax.rem(column + 1, columns)}
     last_column = {"gcol": lax.rem(column + columns - 1, columns)}
@@ -202,6 +203,7 @@
     pl.semaphore_wait(barrier, 3 + owners)
     own_d.wait()
     own_x.wait()
+    own_p.start()
 
     def pass_on(ref, send, recv, c):
         @pl.when((c <= column) & has_right)
@@ -462,11 +464,12 @@
                     if e != g:
                         need = jnp.maximum(need, sum((x == e).astype(jnp.int32) for x in there))
     need_ref[0] = need
+    own_p.wait()
     for s, (d, _) in enumerate(slots):
         give_away(s, d).wait()
 
 
-def front_call(row_map, diag, lower, trailing, rows, columns, owners, sure, quarter):
+def front_call(row_map, diag, lower, trailing, parent, rows, columns, owners, sure, quarter):
     n = diag.shape[1]
     share, part = diag.shape[0], lower.shape[0]
     q = part * columns
@@ -476,6 +479,9 @@
     grain = math.gcd(part, BLOCK)
     grains = part // grain
     group = math.gcd(n, 4 * BLOCK)
+    arrays = (
+        diag, lower.reshape(part // grain, grain, n), trailing.reshape(blocks, BLOCK, q), parent
+    )
     return pl.pallas_call(
         functools.partial(front_kernel, rows, columns, owners, sure, quarter),
         name="front",
@@ -483,10 +489,11 @@
             jax.ShapeDtypeStruct((share, n), F32),
             jax.ShapeDtypeStruct((part, n), F32),
             jax.ShapeDtypeStruct((blocks + away, BLOCK, q), F32),
+            jax.ShapeDtypeStruct(parent.shape, F32),
             jax.ShapeDtypeStruct((1,), jnp.int32),
         ),
-        in_specs=[SMEM] + [pl.BlockSpec(memory_space=pl.ANY)] * 3,
-        out_specs=(VMEM,) * 3 + (SMEM,),
+        in_specs=[SMEM] + [pl.BlockSpec(memory_space=pltpu.HBM)] * 4,
+        out_specs=(VMEM,) * 4 + (SMEM,),
         scratch_shapes=[
             pltpu.VMEM((n, n), F32),
             pltpu.VMEM((n // BLOCK, BLOCK, BLOCK), F32),
@@ -503,17 +510,15 @@
             pltpu.VMEM((blocks, BLOCK, q), F32),
             pltpu.VMEM((away, BLOCK, q), F32),
             dma((away,)), dma((away,)),
-            dma((3,)), dma((2, 2, columns)), dma((2, columns)), dma((2, columns)), dma((2, columns)),
+            dma((4,)), dma((2, 2, columns)), dma((2, columns)), dma((2, columns)), dma((2, columns)),
             dma((2, 2, columns)), dma((2, 2, columns)),
             dma((grains, 2, columns)), dma((grains, columns)),
             dma((grains, 2, columns)), dma((grains, columns)),
         ],
         compiler_params=pltpu.CompilerParams(
-            vmem_limit_bytes=56 << 20, collective_id=0, has_side_effects=True
+            vmem_limit_bytes=40 << 20, collective_id=0, has_side_effects=True
         ),
-    )(
-        row_map, diag, lower.reshape(part // grain, grain, n), trailing.reshape(blocks, BLOCK, q)
-    )
+    )(row_map, *(pltpu.with_memory_space_constraint(x, pltpu.HBM) for x in arrays))
 
 
 def rest_kernel(owners, sure, more, quarter, map_ref, piece_ref, out_ref, stage, send, recv):
@@ -567,8 +572,8 @@
 
 
 def add_kernel(owners, sure, more, map_ref, parent_ref, factor_ref, panel_ref, *refs):
-    pieces = refs[:-6]
-    out_ref, factor_out, panel_out, total, read, write = refs[-6:]
+    pieces = refs[:-5]
+    out_ref, factor_out, panel_out, total, write = refs[-5:]
     per_owner = total.shape[0] // BLOCK
     quarter = owners * per_owner
     q = pieces[0].shape[2]
@@ -580,21 +585,16 @@
     def rows_of(p):
         return pl.ds(pl.multiple_of(p * BLOCK, BLOCK), BLOCK)
 
-    def fetch(p):
-        return pltpu.make_async_copy(parent_ref.at[rows_of(p)], total.at[rows_of(p)], read.at[p])
-
     def store(p):
         return pltpu.make_async_copy(total.at[rows_of(p)], out_ref.at[rows_of(p)], write.at[p])
 
-    for p in range(per_owner):
-        fetch(p).start()
     others = (
         pltpu.make_async_copy(factor_ref, factor_out, write.at[per_owner]),
         pltpu.make_async_copy(panel_ref, panel_out, write.at[per_owner + 1]),
     )
 
     def add_rows(p, carry):
-        fetch(p).wait()
+        total[rows_of(p), :] = parent_ref[rows_of(p), :]
 
         def add(g, carry):
             block, slot, rank = jnp.int32(-1), jnp.int32(-1), jnp.int32(0)
@@ -645,9 +645,9 @@
         functools.partial(add_kernel, owners, sure, more),
         name="extend_add",
         out_shape=tuple(jax.ShapeDtypeStruct(x.shape, F32) for x in (parent, factor, panel)),
-        in_specs=[SMEM, anywhere] + [VMEM] * (2 + len(pieces)),
+        in_specs=[SMEM] + [VMEM] * (3 + len(pieces)),
         out_specs=(anywhere,) * 3,
-        scratch_shapes=[pltpu.VMEM(parent.shape, F32), dma((per_owner,)), dma((per_owner + 2,))],
+        scratch_shapes=[pltpu.VMEM(parent.shape, F32), dma((per_owner + 2,))],
         compiler_params=pltpu.CompilerParams(vmem_limit_bytes=24 << 20),
     )(row_map, parent, factor, panel, *pieces)
 
@@ -659,15 +659,16 @@
     blocks = trailing_block.shape[1] // BLOCK
     most = most_slots(blocks, quarter // owners)
     sure = max(1, 2 * most // 3)
-    factor, panel, pieces, need = front_call(
-        row_map, diag_block[0], lower_block[0], trailing_block[0], rows, columns, owners, sure, quarter,
+    factor, panel, pieces, held, need = front_call(
+        row_map, diag_block[0], lower_block[0], trailing_block[0], parent_front[0],
+        rows, columns, owners, sure, quarter,
     )
 
     def finish(more):
         def run():
             extra = (rest_call(row_map, pieces, owners, sure, more, quarter),) if more else ()
             return add_call(
-                row_map, parent_front[0], factor, panel, (pieces,) + extra, owners, sure, more
+                row_map, held, factor, panel, (pieces,) + extra, owners, sure, more
             )
 
         return run

time: 141 us -> 138 us (0.979)
  Pallas kernels: 139 us -> 136 us
    pallas_call x1, Pallas kernels: 7.73 us -> 4.52 us  [add_call(): pl.pallas_call(functools.partial(add_kernel, owners, sure, more), name='e...]
where the time goes in v1:
time: 138 us; the launch traced here: 137 us
  Pallas kernels  136 us (99%)
    pallas_call x1, Pallas kernels, front_call(): pl.pallas_call(functools.partial(front_kernel, rows, columns, owners, sur...  119 us
    pallas_call x1, Pallas kernels, rest_call(): pl.pallas_call(functools.partial(rest_kernel, owners, sure, more, quarter...  12.3 us
    pallas_call x1, Pallas kernels, add_call(): pl.pallas_call(functools.partial(add_kernel, owners, sure, more), name='e...  4.52 us

profile of v1, /device:TPU:4, one launch (start us, length us, event | category | flops | bytes accessed | tf_op | source)
XLA Modules:
  0.0 137.4 jit_solution(1321181218256556199)
XLA Ops:
  0.6 0.0 copy-start
  0.6 119.1 %front.1 = (f32[64,1024]{1,0:T(8,128)S(1)}, f32[192,1024]{1,0:T(8,128)S(1)}, f32[10,128,768]{2,1,0:T(8,128)S(1)}, f32[1024,2048]{1,0:T(8,128)S(1)}, s32[1]{0:T(128)}) custom-call(s32[2,24]{1,0:T(2,128)} %map_ref.1, f32[64,1024]{1,0:T(8,128)} %bitcast.17, f32[3,64,1024]{2,1,0:T(8,128)} %bitcast.16, f32[6,128,768]{2,1,0:T(8,128)} %bitcast.15, ...), custom_call_target="tpu_custom_call" | custom-call | tf_op jit(solution)/shard_map/front/pallas_call | solution.py:485
  120.4 0.0 copy-done
  120.4 16.8 %conditional.1 = (f32[1,64,1024]{2,1,0:T(8,128)}, f32[1,192,1024]{2,1,0:T(8,128)}, f32[1,1024,2048]{2,1,0:T(8,128)}) conditional(s32[]{:T(128)} %bitcast.13, (s32[2,24]{1,0:T(2,128)S(1)}, f32[1024,2048]{1,0:T(8,128)S(1)}, f32[64,1024]{1,0:T(8,128)S(1)}, f32[192,1024]{1,0:T(8,128)S(1)}, f32[10,128,768]{2,1,0:T(8,128)S(1)}) %tuple.45, ...), branch_computations={%region_0.1_spmd, %region_1.2_spmd, %region_2.3_spmd} | conditional | bytes 24 | solution.py:677
  120.4 12.3 %rest.2.refs_1_ = f32[1,128,768]{2,1,0:T(8,128)S(1)} custom-call(s32[2,24]{1,0:T(2,128)S(1)} %get-tuple-element.51.map_ref, f32[10,128,768]{2,1,0:T(8,128)S(1)} %get-tuple-element.55.piece_ref.refs_0_), custom_call_target="tpu_custom_call" | custom-call | tf_op jit(solution)/shard_map/cond/branch_1_fun/rest/pallas_call | solution.py:561
  132.7 4.5 %extend_add.4 = (f32[1024,2048]{1,0:T(8,128)}, f32[64,1024]{1,0:T(8,128)}, f32[192,1024]{1,0:T(8,128)}) custom-call(s32[2,24]{1,0:T(2,128)S(1)} %get-tuple-element.51.map_ref, f32[1024,2048]{1,0:T(8,128)S(1)} %get-tuple-element.52.parent_ref, f32[64,1024]{1,0:T(8,128)S(1)} %get-tuple-element.53.factor_ref, f32[192,1024]{1,0:T(8,128)S(1)} %get-tuple-element.54.panel_ref, ...), custom_call_target="tpu_custom_call" | custom-call | tf_op jit(solution)/shard_map/cond/branch_1_fun/extend_add/pallas_call | solution.py:644
Async XLA Ops:
  0.6 119.7 %copy-start = (s32[2,24]{1,0:T(2,128)S(1)}, s32[2,24]{1,0:T(2,128)}, u32[]{:S(2)}) copy-start(s32[2,24]{1,0:T(2,128)} %map_ref.1) | copy-start | bytes 580

commit v2 on v1

--- a/solution.py
+++ b/solution.py
@@ -130,6 +130,10 @@
     return min(blocks, per_owner)
 
 
+def lends(owners, sure, most, rows):
+    return owners == 2 and sure == 4 and sure < most <= sure + 2 and rows % 2 == 0
+
+
 def invert_diagonal(l_ref, w_ref, wh, wl):
     group = wh.shape[1]
 
@@ -149,8 +153,8 @@
 def front_kernel(
     rows, columns, owners, sure, quarter, map_ref, d_ref, x_ref, t_ref, parent_ref,
     factor_ref, panel_ref, piece_ref, held_ref, need_ref,
-    a, w, br, bc, xh, xl, yh, yl, lh, ll, wh, wl, t, stage, x_send, x_recv,
-    local, line_send, line_recv, far_send, far_recv, near_send, near_recv,
+    a, w, br, bc, xh, xl, yh, yl, lh, ll, wh, wl, t, stage, cand, lent, x_send, x_recv,
+    o_send, o_recv, f_send, f_recv, local, line_send, line_recv, far_send, far_recv, near_send, near_recv,
     b_send, b_recv, c_send, c_recv,
 ):
     child = lax.axis_index("wide")
@@ -421,19 +425,53 @@
         )
 
     slots = [(d, i) for d in range(1, owners) for i in range(sure)]
-    picked = [pick(lax.rem(child + d, owners), i) for d, i in slots]
+    lend = lends(owners, sure, most_slots(blocks, per_owner), rows)
+    rank_at = (0, 2, 3, 1) if lend else tuple(range(sure))
+    picked = [pick(lax.rem(child + d, owners), rank_at[i]) for d, i in slots]
     each = BLOCK // grain
     columns_side = tuple(x[...].reshape(q, n) for x in (xh, xl))
-    for first in range(0, len(slots), 2):
-        group = picked[first : first + 2]
+
+    def moved(group):
         sides = tuple(
             jnp.concatenate([y[block * each + h] for block in group for h in range(each)], axis=0)
             for y in (yh, yl)
         )
         product = split_dot(sides, columns_side, NT)
-        for e, block in enumerate(group):
-            stage[first + e] = t[block] - product[e * BLOCK : e * BLOCK + BLOCK, :]
-            give_away(first + e, slots[first + e][0]).start()
+        return [t[b] - product[e * BLOCK : e * BLOCK + BLOCK, :] for e, b in enumerate(group)]
+
+    def lend_on(o):
+        return pltpu.make_async_remote_copy(
+            src_ref=lent.at[o], dst_ref=cand.at[2 * o + 1], send_sem=o_send.at[o],
+            recv_sem=o_recv.at[o], device_id=near, device_id_type=pl.DeviceIdType.MESH,
+        )
+
+    def hand_back(o):
+        return pltpu.make_async_remote_copy(
+            src_ref=piece_ref.at[blocks + 2 - o], dst_ref=piece_ref.at[blocks + sure + o],
+            send_sem=f_send.at[o], recv_sem=f_recv.at[o], device_id=near,
+            device_id_type=pl.DeviceIdType.MESH,
+        )
+
+    if lend:
+        to = lax.rem(child + 1, owners)
+        count = sum((x == to).astype(jnp.int32) for x in mine)
+        stage[0], lent[0] = moved([picked[0], pick(to, sure)])
+        give_away(0, 1).start()
+        lend_on(0).start()
+        lent[1], cand[2] = moved([pick(to, sure + 1), picked[1]])
+        lend_on(1).start()
+        cand[0], stage[3] = moved([picked[2], picked[3]])
+        for o in range(2):
+            lend_on(o).wait()
+        for o in range(2):
+            stage[2 - o] = cand[2 * o + jnp.where(count > 3 - o, 0, 1)]
+        for s in (1, 2, 3):
+            give_away(s, 1).start()
+    else:
+        for first in range(0, len(slots), 2):
+            for e, value in enumerate(moved(picked[first : first + 2])):
+                stage[first + e] = value
+                give_away(first + e, slots[first + e][0]).start()
     step = 3 if blocks % 3 == 0 else 1
     for first in range(0, blocks, step):
         rows_side = tuple(
@@ -458,15 +496,35 @@
     need = jnp.int32(0)
     if sure < most_slots(blocks, per_owner):
         for g in range(owners):
+            counts = [
+                [
+                    sum((x == e).astype(jnp.int32) for x in there)
+                    for e in range(owners)
+                    if e != g
+                ]
+                for there in ([owner(g, r, b) for b in range(blocks)] for r in range(rows))
+            ]
             for r in range(rows):
-                there = [owner(g, r, b) for b in range(blocks)]
-                for e in range(owners):
-                    if e != g:
-                        need = jnp.maximum(need, sum((x == e).astype(jnp.int32) for x in there))
+                for e, k in enumerate(counts[r]):
+                    if lend:
+                        beside = counts[r + 1 - 2 * (r % 2)][e]
+                        stuck = (k > sure) & (beside > 3) | (k > sure + 1) & (beside > 2)
+                        k = jnp.where(stuck, k, 0)
+                    need = jnp.maximum(need, k)
     need_ref[0] = need
     own_p.wait()
+    if lend:
+        for o in (1, 0):
+            give_away(2 - o, 1).wait_recv()
+            hand_back(o).start()
     for s, (d, _) in enumerate(slots):
-        give_away(s, d).wait()
+        if lend and s in (1, 2):
+            give_away(s, d).wait_send()
+        else:
+            give_away(s, d).wait()
+    if lend:
+        for o in range(2):
+            hand_back(o).wait()
 
 
 def front_call(row_map, diag, lower, trailing, parent, rows, columns, owners, sure, quarter):
@@ -479,6 +537,8 @@
     grain = math.gcd(part, BLOCK)
     grains = part // grain
     group = math.gcd(n, 4 * BLOCK)
+    most = most_slots(blocks, quarter // owners)
+    extra = 2 if lends(owners, sure, most, rows) else 0
     arrays = (
         diag, lower.reshape(part // grain, grain, n), trailing.reshape(blocks, BLOCK, q), parent
     )
@@ -488,7 +548,7 @@
         out_shape=(
             jax.ShapeDtypeStruct((share, n), F32),
             jax.ShapeDtypeStruct((part, n), F32),
-            jax.ShapeDtypeStruct((blocks + away, BLOCK, q), F32),
+            jax.ShapeDtypeStruct((blocks + away + extra, BLOCK, q), F32),
             jax.ShapeDtypeStruct(parent.shape, F32),
             jax.ShapeDtypeStruct((1,), jnp.int32),
         ),
@@ -509,7 +569,10 @@
             pltpu.VMEM((n // group, group, group), BF16),
             pltpu.VMEM((blocks, BLOCK, q), F32),
             pltpu.VMEM((away, BLOCK, q), F32),
+            pltpu.VMEM((2 * max(extra, 1), BLOCK, q), F32),
+            pltpu.VMEM((max(extra, 1), BLOCK, q), F32),
             dma((away,)), dma((away,)),
+            dma((2,)), dma((2,)), dma((2,)), dma((2,)),
             dma((4,)), dma((2, 2, columns)), dma((2, columns)), dma((2, columns)), dma((2, columns)),
             dma((2, 2, columns)), dma((2, 2, columns)),
             dma((grains, 2, columns)), dma((grains, columns)),
@@ -571,7 +634,7 @@
     )(row_map, pieces)
 
 
-def add_kernel(owners, sure, more, map_ref, parent_ref, factor_ref, panel_ref, *refs):
+def add_kernel(owners, sure, more, lend, map_ref, parent_ref, factor_ref, panel_ref, *refs):
     pieces = refs[:-5]
     out_ref, factor_out, panel_out, total, write = refs[-5:]
     per_owner = total.shape[0] // BLOCK
@@ -612,15 +675,29 @@
                     at = pl.ds(pl.multiple_of(to * BLOCK, BLOCK), BLOCK)
                     total[rows_of(p), at] += ref[index, :, b * BLOCK : b * BLOCK + BLOCK]
 
-            @pl.when((block >= 0) & ((g == child) | (slot < sure)))
+            over = slot - sure
+            place = blocks + away * sure + slot
+            direct = (g == child) | (over < 0)
+            if lend:
+                beside_row = row + 1 - 2 * lax.rem(row, 2)
+                beside = jnp.int32(0)
+                for b in range(blocks):
+                    to = map_ref[g, beside_row * blocks + b] % quarter
+                    beside += (to // per_owner == child).astype(jnp.int32)
+                place = blocks + jnp.where(
+                    slot == 1, 3, jnp.where((slot == 2) | (slot == 3), slot - 1, slot)
+                )
+                direct = direct | (beside + over < 4)
+
+            @pl.when((block >= 0) & direct)
             def _():
-                put(pieces[0], jnp.where(g == child, block, blocks + away * sure + slot))
+                put(pieces[0], jnp.where(g == child, block, place))
 
             if len(pieces) > 1:
 
-                @pl.when((block >= 0) & (g != child) & (slot >= sure))
+                @pl.when((block >= 0) & jnp.logical_not(direct))
                 def _():
-                    put(pieces[1], away * more + slot - sure)
+                    put(pieces[1], away * more + over)
 
             return carry
 
@@ -637,12 +714,12 @@
         copy.wait()
 
 
-def add_call(row_map, parent, factor, panel, pieces, owners, sure, more):
+def add_call(row_map, parent, factor, panel, pieces, owners, sure, more, lend):
     dma = pltpu.SemaphoreType.DMA
     per_owner = parent.shape[0] // BLOCK
     anywhere = pl.BlockSpec(memory_space=pl.ANY)
     return pl.pallas_call(
-        functools.partial(add_kernel, owners, sure, more),
+        functools.partial(add_kernel, owners, sure, more, lend),
         name="extend_add",
         out_shape=tuple(jax.ShapeDtypeStruct(x.shape, F32) for x in (parent, factor, panel)),
         in_specs=[SMEM] + [VMEM] * (3 + len(pieces)),
@@ -659,6 +736,7 @@
     blocks = trailing_block.shape[1] // BLOCK
     most = most_slots(blocks, quarter // owners)
     sure = max(1, 2 * most // 3)
+    lend = lends(owners, sure, most, rows)
     factor, panel, pieces, held, need = front_call(
         row_map, diag_block[0], lower_block[0], trailing_block[0], parent_front[0],
         rows, columns, owners, sure, quarter,
@@ -668,7 +746,7 @@
         def run():
             extra = (rest_call(row_map, pieces, owners, sure, more, quarter),) if more else ()
             return add_call(
-                row_map, held, factor, panel, (pieces,) + extra, owners, sure, more
+                row_map, held, factor, panel, (pieces,) + extra, owners, sure, more, lend
             )
 
         return run

time: 138 us -> 127 us (0.920)
  Pallas kernels: 136 us -> 124 us
    pallas_call x2 -> x1, Pallas kernels: 16.8 us -> 5.21 us  [add_call(): pl.pallas_call(functools.partial(add_kernel, owners, sure, more, lend), n...]
where the time goes in v2:
time: 127 us; the launch traced here: 126 us
  Pallas kernels  124 us (98%)
  between operations  1.38 us (1%)
    pallas_call x1, Pallas kernels, front_call(): pl.pallas_call(functools.partial(front_kernel, rows, columns, owners, sur...  119 us
    pallas_call x1, Pallas kernels, add_call(): pl.pallas_call(functools.partial(add_kernel, owners, sure, more, lend), n...  5.21 us

profile of v2, /device:TPU:4, one launch (start us, length us, event | category | flops | bytes accessed | tf_op | source)
XLA Modules:
  0.0 125.8 jit_solution(3324198200427216460)
XLA Ops:
  0.6 0.0 copy-start
  0.6 119.2 %front.1 = (f32[64,1024]{1,0:T(8,128)S(1)}, f32[192,1024]{1,0:T(8,128)S(1)}, f32[12,128,768]{2,1,0:T(8,128)S(1)}, f32[1024,2048]{1,0:T(8,128)S(1)}, s32[1]{0:T(128)}) custom-call(s32[2,24]{1,0:T(2,128)} %map_ref.1, f32[64,1024]{1,0:T(8,128)} %bitcast.17, f32[3,64,1024]{2,1,0:T(8,128)} %bitcast.16, f32[6,128,768]{2,1,0:T(8,128)} %bitcast.15, ...), custom_call_target="tpu_custom_call" | custom-call | tf_op jit(solution)/shard_map/front/pallas_call | solution.py:545
  120.4 0.0 copy-done
  120.5 5.2 %conditional.1 = (f32[1,64,1024]{2,1,0:T(8,128)}, f32[1,192,1024]{2,1,0:T(8,128)}, f32[1,1024,2048]{2,1,0:T(8,128)}) conditional(s32[]{:T(128)} %bitcast.13, (s32[2,24]{1,0:T(2,128)S(1)}, f32[1024,2048]{1,0:T(8,128)S(1)}, f32[64,1024]{1,0:T(8,128)S(1)}, f32[192,1024]{1,0:T(8,128)S(1)}, f32[12,128,768]{2,1,0:T(8,128)S(1)}) %tuple.45, ...), branch_computations={%region_0.1_spmd, %region_1.2_spmd, %region_2.3_spmd} | conditional | bytes 24 | solution.py:755
  120.5 5.2 %extend_add.3 = (f32[1024,2048]{1,0:T(8,128)}, f32[64,1024]{1,0:T(8,128)}, f32[192,1024]{1,0:T(8,128)}) custom-call(s32[2,24]{1,0:T(2,128)S(1)} %get-tuple-element.46.map_ref, f32[1024,2048]{1,0:T(8,128)S(1)} %get-tuple-element.47.parent_ref, f32[64,1024]{1,0:T(8,128)S(1)} %get-tuple-element.48.factor_ref, f32[192,1024]{1,0:T(8,128)S(1)} %get-tuple-element.49.panel_ref, ...), custom_call_target="tpu_custom_call" | custom-call | tf_op jit(solution)/shard_map/cond/branch_0_fun/extend_add/pallas_call | solution.py:721
Async XLA Ops:
  0.6 119.8 %copy-start = (s32[2,24]{1,0:T(2,128)S(1)}, s32[2,24]{1,0:T(2,128)}, u32[]{:S(2)}) copy-start(s32[2,24]{1,0:T(2,128)} %map_ref.1) | copy-start | bytes 580
